TPU v7x, 32 devices: a whole 2x2x4 slice. The times are simulated.
32 devices in a mesh: groups: 1, frames: 32 (over z, y, x, core).
Axes of the slice: x: 2, y: 2, z: 4, core: 2. Of those that a mesh axis runs over, the one named last changes fastest.
Arguments:
- skip: bfloat16 [32, 256, 640], P(('groups', 'frames')), may hold values from -24 to 24
- control: bfloat16 [32, 256, 640], P('groups', 'frames'), may hold values from -6 to 6
- zero_weight: bfloat16 [640, 640], replicated, may hold values from -1 to 1
- gn_gain: float32 [640], replicated, may hold values from 0.1 to 1.9
- gn_bias: float32 [640], replicated, may hold values from -0.5 to 0.5
- conv_weight: bfloat16 [9, 640, 640], replicated, may hold values from -0.078125 to 0.078125
- ln_gain: float32 [640], replicated, may hold values from 0.1 to 1.9
- qkv_weight: bfloat16 [640, 1920], replicated, may hold values from -5 to 5
- out_weight: bfloat16 [640, 640], replicated, may hold values from -0.25 to 0.25
Outputs:
- output: bfloat16 [32, 256, 640], P(('groups', 'frames'))
All inputs are finite; a program needn't handle non-finite values.
Results may differ from a plain program's by a relative error of at most 0.0043.
Values may be sent and summed in bfloat16 or wider, within the bound.
No kernel may reach another device: no remote copies, remote signals or barrier semaphores. Data moves between devices by JAX's collectives and lax.ppermute only.
A program may use at most 64 MiB of HBM per device.

v0:
```python
import math
import jax
import jax.numpy as jnp
from jax import lax
from jax.sharding import PartitionSpec as P

HEADS = 10
HD = 64
GROUPS = 32
CLIP = 32
W = 32
norm_epsilon = 1e-05


def attend_block(qkv_rows, chans):
    frame_count, single, count, _ = qkv_rows.shape
    clip_count = frame_count // CLIP
    shaped = qkv_rows.reshape(clip_count, CLIP, count, 3, HEADS, HD)
    queries = shaped[:, :, :, 0]
    key_rows = shaped[:, :, :, 1]
    value_rows = shaped[:, :, :, 2]
    scores = jnp.einsum(
        "atphd,asphd->aphts", queries, key_rows, preferred_element_type=jnp.float32
    ) * (1.0 / math.sqrt(HD))
    scores = scores - jnp.max(scores, axis=-1, keepdims=True)
    expon = jnp.exp(scores)
    attn_weights = (expon / jnp.sum(expon, axis=-1, keepdims=True)).astype(jnp.bfloat16)
    mixed = jnp.einsum(
        "aphts,asphd->atphd", attn_weights, value_rows, preferred_element_type=jnp.float32
    )
    return mixed.astype(jnp.bfloat16).reshape(frame_count, single, count, chans)


def body(
    skip, control, zero_weight, gn_gain, gn_bias, conv_weight, ln_gain, qkv_weight, out_weight
):
    f_dev, pixels, chans = skip.shape
    devices = lax.axis_size("frames")
    frame_count, pix_dev, _ = control.shape
    height = pixels // W
    zero_out = jnp.dot(control.reshape(-1, chans), zero_weight, preferred_element_type=jnp.float32)
    zero_out = zero_out.astype(jnp.bfloat16).reshape(frame_count, pix_dev, chans)
    zero_frames = lax.all_to_all(zero_out, "frames", split_axis=0, concat_axis=1, tiled=True)
    joined = skip.astype(jnp.float32) + zero_frames.astype(jnp.float32)
    group_size = chans // GROUPS
    grouped = joined.reshape(f_dev, pixels, GROUPS, group_size)
    clip_count = f_dev * devices // CLIP
    frame_ids = lax.axis_index("frames") * f_dev + jnp.arange(f_dev, dtype=jnp.int32)
    member = (
        frame_ids[:, None] // CLIP == jnp.arange(clip_count, dtype=jnp.int32)[None, :]
    ).astype(jnp.float32)
    count_all = float(CLIP * pixels * group_size)
    frame_sums = jnp.sum(grouped, axis=(1, 3))
    clip_sums = jnp.sum(member[:, :, None] * frame_sums[:, None, :], axis=0)
    frame_sq = jnp.sum(jnp.square(grouped), axis=(1, 3))
    clip_sq = jnp.sum(member[:, :, None] * frame_sq[:, None, :], axis=0)
    total_sums, total_sq = lax.psum((clip_sums, clip_sq), "frames")
    clip_mean = total_sums / count_all
    clip_var = total_sq / count_all - jnp.square(clip_mean)
    frame_mean = jnp.sum(member[:, :, None] * clip_mean[None], axis=1)
    centred = grouped - frame_mean[:, None, :, None]
    frame_var = jnp.sum(member[:, :, None] * clip_var[None], axis=1)
    normed_groups = (centred * lax.rsqrt(frame_var + norm_epsilon)[:, None, :, None]).reshape(
        f_dev, pixels, chans
    )
    activated = (
        jax.nn.silu(normed_groups * gn_gain + gn_bias)
        .astype(jnp.bfloat16)
        .reshape(f_dev, height, W, chans)
    )
    padded = jnp.pad(activated, ((0, 0), (1, 1), (1, 1), (0, 0)))
    conv_sum = jnp.zeros((f_dev * pixels, chans), jnp.float32)
    for tap_index in range(9):
        row_shift, col_shift = divmod(tap_index, 3)
        window = padded[:, row_shift : row_shift + height, col_shift : col_shift + W, :].reshape(
            -1, chans
        )
        conv_sum = conv_sum + jnp.dot(
            window, conv_weight[tap_index], preferred_element_type=jnp.float32
        )
    resid = joined.reshape(-1, chans) + conv_sum
    token_mean = jnp.mean(resid, axis=-1, keepdims=True)
    token_var = jnp.mean(jnp.square(resid - token_mean), axis=-1, keepdims=True)
    normed = ((resid - token_mean) * lax.rsqrt(token_var + norm_epsilon) * ln_gain).astype(
        jnp.bfloat16
    )
    per_device = pixels // devices
    qkv_rows = jnp.dot(normed, qkv_weight, preferred_element_type=jnp.float32).astype(jnp.bfloat16)
    qkv_rows = qkv_rows.reshape(f_dev, devices, per_device, 3 * chans)
    attended = attend_block(
        lax.all_to_all(qkv_rows, "frames", split_axis=1, concat_axis=0, tiled=True), chans
    )
    returned = lax.all_to_all(attended, "frames", split_axis=0, concat_axis=1, tiled=True)
    output = resid + jnp.dot(
        returned.reshape(-1, chans), out_weight, preferred_element_type=jnp.float32
    )
    return output.astype(jnp.bfloat16).reshape(f_dev, pixels, chans)


def solution(mesh):
    in_specs = (
        P(("groups", "frames"), None, None),
        P("groups", "frames", None),
        P(),
        P(),
        P(),
        P(),
        P(),
        P(),
        P(),
    )
    out_specs = P(("groups", "frames"), None, None)
    return jax.shard_map(body, mesh=mesh, in_specs=in_specs, out_specs=out_specs, check_vma=False)
```

profile of v0, /device:TPU:0, one launch (start us, length us, event | category | flops | bytes accessed | tf_op | source)
XLA Modules:
  0.0 136.1 jit_solution(5476533162441262583)
XLA Ops:
  0.0 2.6 %fusion.7 = bf16[32,8,640]{2,1,0:T(8,128)(2,1)} fusion(bf16[640,640]{1,0:T(8,128)(2,1)} %param.11, bf16[32,8,640]{2,1,0:T(8,128)(2,1)} %param.10), kind=kOutput, calls=%fused_computation.21 | convolution fusion | flops 209879040 | bytes 1474560 | tf_op jit(solution)/shard_map/dot_general | solution.py:41
  2.6 7.3 %all-to-all-start = ((bf16[32,8,640]{2,1,0:T(8,128)(2,1)}), bf16[32,8,640]{2,1,0:T(8,128)(2,1)S(1)}, u32[]{:S(2)}, u32[]{:S(2)}) async-start(bf16[32,8,640]{2,1,0:T(8,128)(2,1)} %fusion.7), calls=%async_computation | async-start | bytes 655360 | tf_op jit(solution)/shard_map/all_to_all | solution.py:43
  9.9 12.0 %all-to-all-done = bf16[32,8,640]{2,1,0:T(8,128)(2,1)S(1)} async-done(((bf16[32,8,640]{2,1,0:T(8,128)(2,1)}), bf16[32,8,640]{2,1,0:T(8,128)(2,1)S(1)}, u32[]{:S(2)}, u32[]{:S(2)}) %all-to-all-start) | async-done | bytes 327712 | tf_op jit(solution)/shard_map/all_to_all | solution.py:43
  22.0 1.1 multiply_reduce_fusion.1
  23.2 0.1 reduce_sum.76
  23.3 0.1 reduce_sum.80
  23.4 0.1 reduce_sum.77
  23.5 38.5 %all-reduce.1 = (f32[1,32]{1,0:T(1,128)S(1)}, f32[1,32]{1,0:T(1,128)S(1)}) all-reduce(f32[1,32]{1,0:T(1,128)S(1)} %get-tuple-element.27, f32[1,32]{1,0:T(1,128)S(1)} %get-tuple-element.26), channel_id=1, replica_groups=mesh['groups'=1,'frames'=32] {'frames'}, use_global_device_ids=true, to_apply=%region_2.3 | all-reduce | flops 64 | bytes 512 | tf_op jit(solution)/shard_map/psum | solution.py:57
  62.1 0.1 sub.46
  62.3 0.1 mul.145
  62.4 1.1 multiply_convert_fusion.1
  63.5 0.3 pad_slice_fusion
  63.8 2.0 %fusion.17 = f32[256,640]{1,0:T(8,128)S(1)} fusion(bf16[256,640]{1,0:T(8,128)(2,1)S(1)} %bitcast.123, bf16[9,640,640]{2,1,0:T(8,128)(2,1)} %param.14), kind=kOutput, calls=%fused_computation.31 | convolution fusion | flops 209715200 | bytes 1802240 | tf_op jit(solution)/shard_map/dot_general | solution.py:78
  65.8 1.6 %convolution_add_fusion.8 = f32[256,640]{1,0:T(8,128)S(1)} fusion(f32[256,640]{1,0:T(8,128)S(1)} %fusion.17, bf16[256,640]{1,0:T(8,128)(2,1)S(1)} %bitcast.122, bf16[9,640,640]{2,1,0:T(8,128)(2,1)} %param.14), kind=kOutput, calls=%fused_computation.17 | convolution fusion | flops 209879040 | bytes 2457600 | tf_op jit(solution)/shard_map/dot_general | solution.py:78
  67.4 0.5 convolution_add_fusion.7
  67.9 0.5 convolution_add_fusion.6
  68.3 0.5 convolution_add_fusion.5
  68.8 0.5 convolution_add_fusion.4
  69.3 0.5 convolution_add_fusion.3
  69.8 0.5 convolution_add_fusion.2
  70.2 0.6 fusion.39
  70.8 0.2 multiply_reduce_fusion
  71.1 1.0 fusion.1
  72.1 28.4 %all_to_all.12 = bf16[1,32,8,1920]{3,2,0,1:T(8,128)(2,1)} all-to-all(bf16[1,32,8,1920]{3,2,0,1:T(8,128)(2,1)S(1)} %fusion.1), channel_id=1, replica_groups=mesh['groups'=1,'frames'=32] {'frames'}, dimensions={1} | all-to-all | bytes 1966080 | tf_op jit(solution)/shard_map/all_to_all | solution.py:91
  100.5 4.4 %reshape.253 = bf16[1,32,8,3,10,64]{5,4,3,2,1,0:T(8,128)(2,1)} reshape(bf16[1,32,8,1920]{3,2,0,1:T(8,128)(2,1)} %all_to_all.12) | data formatting | bytes 1966080 | tf_op jit(solution)/shard_map/reshape | solution.py:18
  104.9 4.2 %fusion.38 = (bf16[1,32,8,1,10,64]{5,4,3,2,1,0:T(8,128)(2,1)}, bf16[1,32,8,1,10,64]{5,4,3,2,1,0:T(8,128)(2,1)}, bf16[1,32,8,1,10,64]{5,4,3,2,1,0:T(8,128)(2,1)}) fusion(bf16[1,32,8,3,10,64]{5,4,3,2,1,0:T(8,128)(2,1)} %reshape.253), kind=kLoop, calls=%fused_computation.74 | loop fusion | bytes 1966080 | tf_op jit(solution)/shard_map/slice | solution.py:21
  109.1 3.8 %fusion.40 = (f32[8,10,32]{2,1,0:T(8,128)S(1)}, f32[8,10,32,32]{2,3,1,0:T(8,128)}) fusion(bf16[1,32,8,1,10,64]{5,4,3,2,1,0:T(8,128)(2,1)} %get-tuple-element.11, bf16[1,32,8,1,10,64]{5,4,3,2,1,0:T(8,128)(2,1)} %get-tuple-element.10), kind=kOutput, calls=%fused_computation.76 | convolution fusion | flops 10731551 | bytes 993280 | tf_op jit(solution)/shard_map/sub | solution.py:25
  112.9 2.3 %fusion.4 = bf16[1,32,8,10,64]{4,1,3,2,0:T(8,128)(2,1)S(1)} fusion(f32[8,10,32,32]{2,3,1,0:T(8,128)} %get-tuple-element.25, bf16[1,32,8,1,10,64]{5,4,3,2,1,0:T(8,128)(2,1)} %get-tuple-element.9, f32[8,10,32]{2,1,0:T(8,128)S(1)} %get-tuple-element.24), kind=kOutput, calls=%fused_computation.8 | convolution fusion | flops 10813440 | bytes 993280 | tf_op jit(solution)/shard_map/aphts,asphd->atphd/dot_general | solution.py:28
  115.1 1.3 copy.21
  116.5 1.8 %reshape.257 = bf16[32,1,8,640]{3,2,0,1:T(8,128)(2,1)S(1)} reshape(bf16[1,32,8,10,64]{4,3,2,1,0:T(8,128)(2,1)} %copy.21) | data formatting | bytes 655360 | tf_op jit(solution)/shard_map/reshape | solution.py:31
  118.3 15.5 %all_to_all.13 = bf16[32,1,8,640]{3,2,1,0:T(8,128)(2,1)S(1)} all-to-all(bf16[32,1,8,640]{3,2,1,0:T(8,128)(2,1)S(1)} %bitcast.116), channel_id=1, replica_groups=mesh['groups'=1,'frames'=32] {'frames'}, dimensions={0} | all-to-all | bytes 655360 | tf_op jit(solution)/shard_map/all_to_all | solution.py:93
  133.8 2.3 %fusion.8 = bf16[1,256,640]{2,1,0:T(8,128)(2,1)} fusion(f32[256,640]{1,0:T(8,128)S(1)} %get-tuple-element.23, bf16[640,640]{1,0:T(8,128)(2,1)} %param.17, bf16[32,1,8,640]{3,2,1,0:T(8,128)(2,1)S(1)} %all_to_all.13), kind=kOutput, calls=%fused_computation.22 | convolution fusion | flops 210042880 | bytes 2129920 | tf_op jit(solution)/shard_map/dot_general | solution.py:94
  (17 shorter events, 0.3 us)
Async XLA Ops:
  0.0 71.0 %copy-start = (bf16[640,1920]{1,0:T(8,128)(2,1)S(1)}, bf16[640,1920]{1,0:T(8,128)(2,1)}, u32[]{:S(2)}) copy-start(bf16[640,1920]{1,0:T(8,128)(2,1)} %param.16) | copy-start | bytes 7372804
  0.0 62.4 %copy-start.2 = (bf16[1,256,640]{2,1,0:T(8,128)(2,1)S(1)}, bf16[1,256,640]{2,1,0:T(8,128)(2,1)}, u32[]{:S(2)}) copy-start(bf16[1,256,640]{2,1,0:T(8,128)(2,1)} %param.9) | copy-start | bytes 983044
  2.6 19.4 %all-to-all-start = ((bf16[32,8,640]{2,1,0:T(8,128)(2,1)}), bf16[32,8,640]{2,1,0:T(8,128)(2,1)S(1)}, u32[]{:S(2)}, u32[]{:S(2)}) async-start(bf16[32,8,640]{2,1,0:T(8,128)(2,1)} %fusion.7), calls=%async_computation | async-start | bytes 655360 | tf_op jit(solution)/shard_map/all_to_all | solution.py:43
  62.4 5.0 %copy-start.1 = (bf16[9,640,640]{2,1,0:T(8,128)(2,1)S(1)}, bf16[9,640,640]{2,1,0:T(8,128)(2,1)}, u32[]{:S(2)}) copy-start(bf16[9,640,640]{2,1,0:T(8,128)(2,1)} %param.14) | copy-start | bytes 22118404
  68.8 1.4 %copy-start.3 = (bf16[1,256,640]{2,1,0:T(8,128)(2,1)S(1)}, bf16[1,256,640]{2,1,0:T(8,128)(2,1)}, u32[]{:S(2)}) copy-start(bf16[1,256,640]{2,1,0:T(8,128)(2,1)} %param.9) | copy-start | bytes 983044
  69.7 1.3 copy-start.4
where the time goes:
time: 137 us; the launch traced here: 136 us
  blocking collectives  82.4 us (60%)
  matrix products  18.8 us (14%)
  local copies, waits for them, and re-layouts  12.6 us (9%)
  waiting for transfers between devices  12 us (9%)
  starting transfers between devices  7.33 us (5%)
  other arithmetic  2.73 us (2%)
    psum x1, blocking collectives, body(): total_sums, total_sq = lax.psum((clip_sums, clip_sq), 'frames')  38.5 us
    all_to_all x1, blocking collectives, body(): lax.all_to_all(qkv_rows, 'frames', split_axis=1, concat_axis=0, tiled=True)  28.4 us
    all_to_all x1, blocking collectives, body(): lax.all_to_all(attended, 'frames', split_axis=0, concat_axis=1, tiled=True)  15.5 us
    all_to_all x1, waiting for transfers between devices, body(): lax.all_to_all(zero_out, 'frames', split_axis=0, concat_axis=1, tiled=True)  12 us
    all_to_all x1, starting transfers between devices, body(): lax.all_to_all(zero_out, 'frames', split_axis=0, concat_axis=1, tiled=True)  7.33 us
    dot_general x9, matrix products, body(): jnp.dot(window, conv_weight[tap_index], preferred_element_type=jnp.float32)  6.89 us
    reshape x1, local copies, waits for them, and re-layouts, attend_block(): shaped = qkv_rows.reshape(clip_count, CLIP, count, 3, HEADS, HD)  4.38 us
    slice x1, local copies, waits for them, and re-layouts, attend_block(): value_rows = shaped[:, :, :, 2]  4.21 us
  transfers between devices with their start and end apart: 1, of which 1 were waited for; matrix products, arithmetic and copies ran while one was open for 0% of the time, Pallas kernels for 0%

commit v1 on v0

--- a/solution.py
+++ b/solution.py
@@ -90,7 +90,10 @@
     attended = attend_block(
         lax.all_to_all(qkv_rows, "frames", split_axis=1, concat_axis=0, tiled=True), chans
     )
-    returned = lax.all_to_all(attended, "frames", split_axis=0, concat_axis=1, tiled=True)
+    n_dev = lax.axis_size("frames")
+    pieces = jnp.stack(jnp.split(attended, n_dev, axis=0), axis=0)
+    pieces = lax.all_to_all(pieces, "frames", split_axis=0, concat_axis=0)
+    returned = jnp.concatenate(pieces, axis=1)
     output = resid + jnp.dot(
         returned.reshape(-1, chans), out_weight, preferred_element_type=jnp.float32
     )

time: 137 us -> 183 us (1.34)
  local copies, waits for them, and re-layouts: 12.6 us -> 57 us
    another operation x0 -> x33, local copies, waits for them, and re-layouts: none -> 28.7 us  [body(): pieces = jnp.stack(jnp.split(attended, n_dev, axis=0), axis=0)]
    unnamed x10 -> x41, local copies, waits for them, and re-layouts: 0.03 us -> 13.6 us
    split x0 -> x2, local copies, waits for them, and re-layouts: none -> 5.28 us  [body(): pieces = jnp.stack(jnp.split(attended, n_dev, axis=0), axis=0)]
    reshape x1 -> x0, local copies, waits for them, and re-layouts: 1.83 us -> none  [attend_block(): return mixed.astype(jnp.bfloat16).reshape(frame_count, single, count, chans)]
where the time goes in v1:
time: 183 us; the launch traced here: 181 us
  blocking collectives  82.4 us (45%)
  local copies, waits for them, and re-layouts  57 us (31%)
  matrix products  18.9 us (10%)
  waiting for transfers between devices  12 us (7%)
  starting transfers between devices  7.32 us (4%)
  other arithmetic  2.73 us (1%)
    psum x1, blocking collectives, body(): total_sums, total_sq = lax.psum((clip_sums, clip_sq), 'frames')  38.5 us
    another operation x33, local copies, waits for them, and re-layouts, body(): pieces = jnp.stack(jnp.split(attended, n_dev, axis=0), axis=0)  28.7 us
    all_to_all x1, blocking collectives, body(): lax.all_to_all(qkv_rows, 'frames', split_axis=1, concat_axis=0, tiled=True)  28.4 us
    all_to_all x1, blocking collectives, body(): pieces = lax.all_to_all(pieces, 'frames', split_axis=0, concat_axis=0)  15.5 us
    unnamed x41, local copies, waits for them, and re-layouts  13.6 us
    all_to_all x1, waiting for transfers between devices, body(): lax.all_to_all(zero_out, 'frames', split_axis=0, concat_axis=1, tiled=True)  12 us
    all_to_all x1, starting transfers between devices, body(): lax.all_to_all(zero_out, 'frames', split_axis=0, concat_axis=1, tiled=True)  7.32 us
    dot_general x9, matrix products, body(): jnp.dot(window, conv_weight[tap_index], preferred_element_type=jnp.float32)  6.9 us
  transfers between devices with their start and end apart: 1, of which 1 were waited for; matrix products, arithmetic and copies ran while one was open for 0% of the time, Pallas kernels for 0%

profile of v1, /device:TPU:0, one launch (start us, length us, event | category | flops | bytes accessed | tf_op | source)
XLA Modules:
  0.0 180.5 jit_solution(1538507992161779389)
XLA Ops:
  0.0 2.6 %fusion.7 = bf16[32,8,640]{2,1,0:T(8,128)(2,1)} fusion(bf16[640,640]{1,0:T(8,128)(2,1)} %param.11, bf16[32,8,640]{2,1,0:T(8,128)(2,1)} %param.10), kind=kOutput, calls=%fused_computation.21 | convolution fusion | flops 209879040 | bytes 1474560 | tf_op jit(solution)/shard_map/dot_general | solution.py:41
  2.6 7.3 %all-to-all-start = ((bf16[32,8,640]{2,1,0:T(8,128)(2,1)}), bf16[32,8,640]{2,1,0:T(8,128)(2,1)S(1)}, u32[]{:S(2)}, u32[]{:S(2)}) async-start(bf16[32,8,640]{2,1,0:T(8,128)(2,1)} %fusion.7), calls=%async_computation | async-start | bytes 655360 | tf_op jit(solution)/shard_map/all_to_all | solution.py:43
  9.9 12.0 %all-to-all-done = bf16[32,8,640]{2,1,0:T(8,128)(2,1)S(1)} async-done(((bf16[32,8,640]{2,1,0:T(8,128)(2,1)}), bf16[32,8,640]{2,1,0:T(8,128)(2,1)S(1)}, u32[]{:S(2)}, u32[]{:S(2)}) %all-to-all-start) | async-done | bytes 327712 | tf_op jit(solution)/shard_map/all_to_all | solution.py:43
  23.5 38.5 %all-reduce.1 = (f32[1,32]{1,0:T(1,128)S(1)}, f32[1,32]{1,0:T(1,128)S(1)}) all-reduce(f32[1,32]{1,0:T(1,128)S(1)} %get-tuple-element.59, f32[1,32]{1,0:T(1,128)S(1)} %get-tuple-element.58), channel_id=1, replica_groups=mesh['groups'=1,'frames'=32] {'frames'}, use_global_device_ids=true, to_apply=%region_2.3 | all-reduce | flops 64 | bytes 512 | tf_op jit(solution)/shard_map/psum | solution.py:57
  63.8 2.0 %fusion.17 = f32[256,640]{1,0:T(8,128)S(1)} fusion(bf16[256,640]{1,0:T(8,128)(2,1)S(1)} %bitcast.121, bf16[9,640,640]{2,1,0:T(8,128)(2,1)} %param.14), kind=kOutput, calls=%fused_computation.31 | convolution fusion | flops 209715200 | bytes 1802240 | tf_op jit(solution)/shard_map/dot_general | solution.py:78
  65.8 1.6 convolution_add_fusion.8
  72.1 28.4 %all_to_all.23 = bf16[1,32,8,1920]{3,2,0,1:T(8,128)(2,1)} all-to-all(bf16[1,32,8,1920]{3,2,0,1:T(8,128)(2,1)S(1)} %fusion.1), channel_id=1, replica_groups=mesh['groups'=1,'frames'=32] {'frames'}, dimensions={1} | all-to-all | bytes 1966080 | tf_op jit(solution)/shard_map/all_to_all | solution.py:91
  100.5 4.4 %reshape.308 = bf16[1,32,8,3,10,64]{5,4,3,2,1,0:T(8,128)(2,1)} reshape(bf16[1,32,8,1920]{3,2,0,1:T(8,128)(2,1)} %all_to_all.23) | data formatting | bytes 1966080 | tf_op jit(solution)/shard_map/reshape | solution.py:18
  104.9 4.2 %fusion.38 = (bf16[1,32,8,1,10,64]{5,4,3,2,1,0:T(8,128)(2,1)}, bf16[1,32,8,1,10,64]{5,4,3,2,1,0:T(8,128)(2,1)}, bf16[1,32,8,1,10,64]{5,4,3,2,1,0:T(8,128)(2,1)}) fusion(bf16[1,32,8,3,10,64]{5,4,3,2,1,0:T(8,128)(2,1)} %reshape.308), kind=kLoop, calls=%fused_computation.138 | loop fusion | bytes 1966080 | tf_op jit(solution)/shard_map/slice | solution.py:21
  109.1 3.8 %fusion.40 = (f32[8,10,32]{2,1,0:T(8,128)S(1)}, f32[8,10,32,32]{2,3,1,0:T(8,128)}) fusion(bf16[1,32,8,1,10,64]{5,4,3,2,1,0:T(8,128)(2,1)} %get-tuple-element.43, bf16[1,32,8,1,10,64]{5,4,3,2,1,0:T(8,128)(2,1)} %get-tuple-element.42), kind=kOutput, calls=%fused_computation.140 | convolution fusion | flops 10731551 | bytes 993280 | tf_op jit(solution)/shard_map/sub | solution.py:25
  112.9 2.3 %fusion.4 = bf16[1,32,8,10,64]{4,1,3,2,0:T(8,128)(2,1)S(1)} fusion(f32[8,10,32,32]{2,3,1,0:T(8,128)} %get-tuple-element.57, bf16[1,32,8,1,10,64]{5,4,3,2,1,0:T(8,128)(2,1)} %get-tuple-element.41, f32[8,10,32]{2,1,0:T(8,128)S(1)} %get-tuple-element.56), kind=kOutput, calls=%fused_computation.8 | convolution fusion | flops 10813440 | bytes 993280 | tf_op jit(solution)/shard_map/aphts,asphd->atphd/dot_general | solution.py:28
  115.1 2.3 %slice_reduce_fusion.19 = (bf16[8,10,64]{2,1,0:T(8,128)(2,1)}, bf16[8,10,64]{2,1,0:T(8,128)(2,1)}, bf16[8,10,64]{2,1,0:T(8,128)(2,1)}, bf16[8,10,64]{2,1,0:T(8,1...) fusion(bf16[1,32,8,10,64]{4,1,3,2,0:T(8,128)(2,1)S(1)} %fusion.4), kind=kLoop, calls=%fused_computation.117 | loop fusion | bytes 266240 | tf_op jit(solution)/shard_map/split | solution.py:94
  117.4 3.0 %slice_reduce_fusion = (bf16[8,10,64]{2,1,0:T(8,128)(2,1)}, bf16[8,10,64]{2,1,0:T(8,128)(2,1)}, bf16[8,10,64]{2,1,0:T(8,128)(2,1)}, bf16[8,10,64]{2,1,0:T(8,128)...) fusion(bf16[1,32,8,10,64]{4,1,3,2,0:T(8,128)(2,1)S(1)} %fusion.4), kind=kLoop, calls=%fused_computation.98 | loop fusion | bytes 389120 | tf_op jit(solution)/shard_map/split | solution.py:94
  121.2 1.4 stack.111
  122.7 1.4 stack.110
  124.1 1.4 stack.109
  125.6 1.4 stack.108
  127.0 1.4 stack.107
  128.5 1.4 stack.106
  129.9 1.4 stack.105
  131.4 1.4 stack.104
  132.8 1.4 stack.103
  134.2 1.5 stack.102
  135.7 1.4 stack.101
  137.1 1.4 stack.100
  138.6 1.4 stack.99
  141.5 1.4 stack.128
  142.9 1.4 stack.127
  144.4 1.4 stack.126
  145.8 1.4 stack.125
  162.7 15.5 %all_to_all.24 = bf16[32,1,1,8,640]{4,3,2,1,0:T(8,128)(2,1)S(1)} all-to-all(bf16[32,1,1,8,640]{4,3,2,1,0:T(8,128)(2,1)S(1)} %constant_dynamic-update-slice_fusion), channel_id=1, replica_groups=mesh['groups'=1,'frames'=32] {'frames'}, dimensions={0} | all-to-all | bytes 655360 | tf_op jit(solution)/shard_map/all_to_all | solution.py:95
  178.2 2.3 %fusion.8 = bf16[1,256,640]{2,1,0:T(8,128)(2,1)} fusion(f32[256,640]{1,0:T(8,128)S(1)} %get-tuple-element.55, bf16[640,640]{1,0:T(8,128)(2,1)} %param.17, bf16[32,1,1,8,640]{4,3,2,1,0:T(8,128)(2,1)S(1)} %all_to_all.24), kind=kOutput, calls=%fused_computation.22 | convolution fusion | flops 210042880 | bytes 2129920 | tf_op jit(solution)/shard_map/dot_general | solution.py:97
  (81 shorter events, 25.7 us)
Async XLA Ops:
  0.0 71.0 %copy-start = (bf16[640,1920]{1,0:T(8,128)(2,1)S(1)}, bf16[640,1920]{1,0:T(8,128)(2,1)}, u32[]{:S(2)}) copy-start(bf16[640,1920]{1,0:T(8,128)(2,1)} %param.16) | copy-start | bytes 7372804
  0.0 62.4 %copy-start.2 = (bf16[1,256,640]{2,1,0:T(8,128)(2,1)S(1)}, bf16[1,256,640]{2,1,0:T(8,128)(2,1)}, u32[]{:S(2)}) copy-start(bf16[1,256,640]{2,1,0:T(8,128)(2,1)} %param.9) | copy-start | bytes 983044
  2.6 19.4 %all-to-all-start = ((bf16[32,8,640]{2,1,0:T(8,128)(2,1)}), bf16[32,8,640]{2,1,0:T(8,128)(2,1)S(1)}, u32[]{:S(2)}, u32[]{:S(2)}) async-start(bf16[32,8,640]{2,1,0:T(8,128)(2,1)} %fusion.7), calls=%async_computation | async-start | bytes 655360 | tf_op jit(solution)/shard_map/all_to_all | solution.py:43
  62.4 5.0 %copy-start.1 = (bf16[9,640,640]{2,1,0:T(8,128)(2,1)S(1)}, bf16[9,640,640]{2,1,0:T(8,128)(2,1)}, u32[]{:S(2)}) copy-start(bf16[9,640,640]{2,1,0:T(8,128)(2,1)} %param.14) | copy-start | bytes 22118404
  68.8 1.4 copy-start.3
  69.7 1.3 copy-start.4
